TPU v7x, 512 devices: a whole 4x8x8 slice. The times are simulated.
512 devices in a mesh: dp: 4 (over x), context: 16 (over z, core), tensor: 8 (over y).
Axes of the slice: x: 4, y: 8, z: 8, core: 2. Of those that a mesh axis runs over, the one named last changes fastest.
Arguments:
- queries: bfloat16 [16384, 8192], P(('dp', 'context', 'tensor')), may hold values from -5 to 5
- keys: bfloat16 [16384, 1024], P(('dp', 'context', 'tensor')), may hold values from -5 to 5
- values: bfloat16 [16384, 1024], P(('dp', 'context', 'tensor')), may hold values from -6 to 6
- grad_out: bfloat16 [16384, 8192], P(('dp', 'context', 'tensor')), may hold values from -6 to 6
- doc_lengths: int32 [4, 32], replicated, may hold values from 1 to 512, 4096 in all within a row
- deal_plan: int32 [16, 4, 8, 4], replicated, may hold values from 0 to 3, each once within a row
Outputs:
- attention_output: bfloat16 [16384, 8192], P(('dp', 'context'), 'tensor')
- query_gradient: bfloat16 [16384, 8192], P(('dp', 'context'), 'tensor')
- key_gradient: bfloat16 [16384, 1024], P(('dp', 'context'), 'tensor')
- value_gradient: bfloat16 [16384, 1024], P(('dp', 'context'), 'tensor')
Inputs may be any that keep to these rules, and one draw needn't show every extreme that they name: Each row of doc_lengths sums to 4096 and its largest entry is exactly 512. `deal_plan`: each row along the last dimension names every replica once.
All inputs are finite; a program needn't handle non-finite values.
Results may differ from a plain program's by a relative error of at most 0.012.
The roundings to bfloat16 on the way count: a program that leaves them out, or rounds other values in their place, can miss the bound.
Values may be sent and summed in bfloat16 or wider, within the bound.
A program may use at most 64 MiB of HBM per device.

v0:
```python
import jax
import jax.numpy as jnp
from jax import lax
from jax.sharding import PartitionSpec as P

HEAD_SIZE = 128
MOST = 512
QUERY_GROUP = 8


masked_score = -1e30


def shifted(x, axis, by):
    length = lax.axis_size(axis)
    pairs = [(i, i + by) for i in range(length) if 0 <= i + by < length]
    return lax.ppermute(x, axis, pairs)


def on_device(queries, keys, values, grad_out, doc_lengths, deal_plan):
    replica = lax.axis_index("dp")
    column = lax.axis_index("context")
    tensor_lane = lax.axis_index("tensor")
    groups = lax.axis_size("dp")
    lane_count = lax.axis_size("tensor")
    sub_rows = queries.shape[0] // groups
    plan_row = deal_plan[column, replica, tensor_lane]
    replica_ids = jnp.arange(groups, dtype=jnp.int32)
    source_block = jnp.sum(
        replica_ids[None, :] * (plan_row[None, :] == replica_ids[:, None]).astype(jnp.int32), axis=1
    )

    def arrange(matrix):
        return jnp.take(matrix.reshape(groups, sub_rows, matrix.shape[1]), source_block, axis=0)

    def spread(matrix):
        lane_width = matrix.shape[2] // lane_count
        return (
            matrix.reshape(groups, sub_rows, lane_count, lane_width)
            .transpose(0, 2, 1, 3)
            .reshape(groups * lane_count, sub_rows, lane_width)
        )

    q_dealt = arrange(queries)
    k_dealt = arrange(keys)
    v_dealt = arrange(values)
    g_dealt = arrange(grad_out)
    delivered = (
        lax.all_to_all(spread(q_dealt), ("dp", "tensor"), split_axis=0, concat_axis=0, tiled=True),
        lax.all_to_all(spread(k_dealt), ("dp", "tensor"), split_axis=0, concat_axis=0, tiled=True),
        lax.all_to_all(spread(v_dealt), ("dp", "tensor"), split_axis=0, concat_axis=0, tiled=True),
        lax.all_to_all(spread(g_dealt), ("dp", "tensor"), split_axis=0, concat_axis=0, tiled=True),
    )
    q_rows, k_rows, v_rows, g_rows = [
        block_part.reshape(block_part.shape[0] * block_part.shape[1], block_part.shape[2])
        for block_part in delivered
    ]
    tok_rows = q_rows.shape[0]
    kv_heads = k_rows.shape[1] // HEAD_SIZE
    score_scale = HEAD_SIZE ** (-0.5)
    reach_count = (MOST - 2) // tok_rows + 1
    lengths_here = jnp.take(doc_lengths, replica, axis=0)
    bounds = jnp.cumsum(lengths_here)

    def segment(positions):
        return jnp.sum((bounds[None, :] <= positions[:, None]).astype(jnp.int32), axis=1)

    offsets = jnp.arange(tok_rows, dtype=jnp.int32)
    query_pos = column * tok_rows + offsets
    query_seg = segment(query_pos)
    stacked = jnp.stack([k_rows, v_rows])
    nearby = [stacked]
    current = stacked
    for distance in range(reach_count):
        current = shifted(current, "context", 1)
        nearby.append(current)
    tile_masks = []
    for distance in range(reach_count + 1):
        key_pos = (column - distance) * tok_rows + offsets
        tile_masks.append(
            (key_pos[None, :] >= 0)
            & (key_pos[None, :] <= query_pos[:, None])
            & (segment(key_pos)[None, :] == query_seg[:, None])
        )
    q_heads = q_rows.reshape(tok_rows, kv_heads, QUERY_GROUP, HEAD_SIZE)
    g_heads = g_rows.reshape(tok_rows, kv_heads, QUERY_GROUP, HEAD_SIZE)

    def scores_of(key_block):
        return score_scale * jnp.einsum(
            "rhgd,khd->hgrk", q_heads, key_block, preferred_element_type=jnp.float32
        )

    def update_stats(running, key_block, tile_mask):
        tile_scores = scores_of(key_block)
        new_max = jnp.maximum(
            running[0], jnp.max(jnp.where(tile_mask, tile_scores, masked_score), axis=-1)
        )
        new_total = running[1] * jnp.exp(running[0] - new_max) + jnp.sum(
            jnp.where(tile_mask, jnp.exp(tile_scores - new_max[..., None]), 0.0), axis=-1
        )
        return (new_max, new_total)

    def keep_stats(running, key_block, tile_mask):
        return running

    run_max = jnp.full((kv_heads, QUERY_GROUP, tok_rows), masked_score, jnp.float32)
    run_sum = jnp.zeros((kv_heads, QUERY_GROUP, tok_rows), jnp.float32)
    for distance in range(reach_count + 1):
        key_block = nearby[distance][0].reshape(tok_rows, kv_heads, HEAD_SIZE)
        run_max, run_sum = lax.cond(
            jnp.any(tile_masks[distance]),
            update_stats,
            keep_stats,
            (run_max, run_sum),
            key_block,
            tile_masks[distance],
        )
    lse = run_max + jnp.log(run_sum)

    def probabilities(tile_scores, tile_mask):
        return jnp.where(tile_mask, jnp.exp(tile_scores - lse[..., None]), 0.0)

    def add_output(out_accum, key_block, value_block, tile_mask):
        weights_b = probabilities(scores_of(key_block), tile_mask).astype(jnp.bfloat16)
        return out_accum + jnp.einsum(
            "hgrk,khd->rhgd", weights_b, value_block, preferred_element_type=jnp.float32
        )

    def keep_output(out_accum, key_block, value_block, tile_mask):
        return out_accum

    out_accum = jnp.zeros((tok_rows, kv_heads, QUERY_GROUP, HEAD_SIZE), jnp.float32)
    for distance in range(reach_count + 1):
        key_block = nearby[distance][0].reshape(tok_rows, kv_heads, HEAD_SIZE)
        value_block = nearby[distance][1].reshape(tok_rows, kv_heads, HEAD_SIZE)
        out_accum = lax.cond(
            jnp.any(tile_masks[distance]),
            add_output,
            keep_output,
            out_accum,
            key_block,
            value_block,
            tile_masks[distance],
        )
    out_heads = out_accum.astype(jnp.bfloat16)
    row_delta = jnp.sum(
        g_heads.astype(jnp.float32) * out_heads.astype(jnp.float32), axis=-1
    ).transpose(1, 2, 0)

    def backward_tile(dq_accum, key_block, value_block, tile_mask):
        tile_probs = probabilities(scores_of(key_block), tile_mask)
        probs_b = tile_probs.astype(jnp.bfloat16)
        dv_part = jnp.einsum("hgrk,rhgd->khd", probs_b, g_heads, preferred_element_type=jnp.float32)
        dprob = jnp.einsum(
            "rhgd,khd->hgrk", g_heads, value_block, preferred_element_type=jnp.float32
        )
        dscore = (score_scale * tile_probs * (dprob - row_delta[..., None])).astype(jnp.bfloat16)
        dq_next = dq_accum + jnp.einsum(
            "hgrk,khd->rhgd", dscore, key_block, preferred_element_type=jnp.float32
        )
        dk_part = jnp.einsum("hgrk,rhgd->khd", dscore, q_heads, preferred_element_type=jnp.float32)
        return (dq_next, dk_part, dv_part)

    def skip_tile(dq_accum, key_block, value_block, tile_mask):
        empty = jnp.zeros((tok_rows, kv_heads, HEAD_SIZE), jnp.float32)
        return (dq_accum, empty, empty)

    dq_accum = jnp.zeros((tok_rows, kv_heads, QUERY_GROUP, HEAD_SIZE), jnp.float32)
    key_terms = []
    for distance in range(reach_count + 1):
        key_block = nearby[distance][0].reshape(tok_rows, kv_heads, HEAD_SIZE)
        value_block = nearby[distance][1].reshape(tok_rows, kv_heads, HEAD_SIZE)
        dq_accum, dk_part, dv_part = lax.cond(
            jnp.any(tile_masks[distance]),
            backward_tile,
            skip_tile,
            dq_accum,
            key_block,
            value_block,
            tile_masks[distance],
        )
        key_terms.append(
            jnp.stack(
                [
                    dk_part.reshape(tok_rows, kv_heads * HEAD_SIZE),
                    dv_part.reshape(tok_rows, kv_heads * HEAD_SIZE),
                ]
            )
        )
    carried = key_terms[reach_count]
    for distance in range(reach_count - 1, -1, -1):
        carried = shifted(carried, "context", -1) + key_terms[distance]
    attention_output = out_heads.reshape(tok_rows, kv_heads * QUERY_GROUP * HEAD_SIZE)
    query_gradient = dq_accum.astype(jnp.bfloat16).reshape(
        tok_rows, kv_heads * QUERY_GROUP * HEAD_SIZE
    )
    key_gradient = carried[0].astype(jnp.bfloat16)
    value_gradient = carried[1].astype(jnp.bfloat16)
    return (attention_output, query_gradient, key_gradient, value_gradient)


def solution(mesh):
    placed = (
        P(("dp", "context", "tensor"), None),
        P(("dp", "context", "tensor"), None),
        P(("dp", "context", "tensor"), None),
        P(("dp", "context", "tensor"), None),
        P(),
        P(),
    )
    return jax.shard_map(
        on_device,
        mesh=mesh,
        in_specs=placed,
        out_specs=(
            P(("dp", "context"), "tensor"),
            P(("dp", "context"), "tensor"),
            P(("dp", "context"), "tensor"),
            P(("dp", "context"), "tensor"),
        ),
        check_vma=False,
    )
```

profile of v0, /device:TPU:213, one launch (start us, length us, event | category | flops | bytes accessed | tf_op | source)
XLA Modules:
  0.0 122.8 jit_solution(17251935516743880098)
XLA Ops:
  0.7 1.0 dynamic-slice_reduce_fusion
  1.8 1.4 %gather_fusion.2 = bf16[4,8,1024]{2,1,0:T(8,128)(2,1)S(1)} fusion(bf16[4,8,1024]{2,1,0:T(8,128)(2,1)} %bitcast.523, s32[1024]{0:T(1024)S(1)} %pad_clamp_fusion), kind=kCustom, calls=%fused_computation.2.clone | custom fusion | bytes 131088 | tf_op jit(solution)/shard_map/jit(_take)/gather | solution.py:34
  3.2 1.4 %gather_fusion = bf16[4,8,1024]{2,1,0:T(8,128)(2,1)S(1)} fusion(bf16[4,8,1024]{2,1,0:T(8,128)(2,1)} %bitcast.524, s32[1024]{0:T(1024)S(1)} %pad_clamp_fusion), kind=kCustom, calls=%fused_computation.clone | custom fusion | bytes 131088 | tf_op jit(solution)/shard_map/jit(_take)/gather | solution.py:34
  4.6 0.7 broadcast_select_fusion.2
  5.3 9.4 %all-to-all-start = ((bf16[32,8,128]{2,1,0:T(8,128)(2,1)}), bf16[32,8,128]{2,1,0:T(8,128)(2,1)S(1)}, u32[]{:S(2)}, u32[]{:S(2)}) async-start(bf16[32,8,128]{2,1,0:T(8,128)(2,1)} %bitcast.149), calls=%async_computation | async-start | bytes 131072 | tf_op jit(solution)/shard_map/all_to_all | solution.py:50
  15.9 4.8 %all-to-all-done = bf16[32,8,128]{2,1,0:T(8,128)(2,1)S(1)} async-done(((bf16[32,8,128]{2,1,0:T(8,128)(2,1)}), bf16[32,8,128]{2,1,0:T(8,128)(2,1)S(1)}, u32[]{:S(2)}, u32[]{:S(2)}) %all-to-all-start) | async-done | bytes 65568 | tf_op jit(solution)/shard_map/all_to_all | solution.py:50
  20.8 6.7 %all-to-all-start.2 = ((bf16[32,8,128]{2,1,0:T(8,128)(2,1)}), bf16[32,8,128]{2,1,0:T(8,128)(2,1)S(1)}, u32[]{:S(2)}, u32[]{:S(2)}) async-start(bf16[32,8,128]{2,1,0:T(8,128)(2,1)} %bitcast.159), calls=%async_computation.2 | async-start | bytes 131072 | tf_op jit(solution)/shard_map/all_to_all | solution.py:51
  27.5 1.1 broadcast_select_fusion
  28.6 4.9 %all-to-all-done.2 = bf16[32,8,128]{2,1,0:T(8,128)(2,1)S(1)} async-done(((bf16[32,8,128]{2,1,0:T(8,128)(2,1)}), bf16[32,8,128]{2,1,0:T(8,128)(2,1)S(1)}, u32[]{:S(2)}, u32[]{:S(2)}) %all-to-all-start.2) | async-done | bytes 65568 | tf_op jit(solution)/shard_map/all_to_all | solution.py:51
  33.5 6.7 %all-to-all-start.1 = ((bf16[32,8,1024]{2,1,0:T(8,128)(2,1)}), bf16[32,8,1024]{2,1,0:T(8,128)(2,1)S(1)}, u32[]{:S(2)}, u32[]{:S(2)}) async-start(bf16[32,8,1024]{2,1,0:T(8,128)(2,1)} %bitcast.154), calls=%async_computation.1 | async-start | bytes 1048576 | tf_op jit(solution)/shard_map/all_to_all | solution.py:49
  40.2 0.7 fusion.131
  41.2 10.7 %all-to-all-done.1 = bf16[32,8,1024]{2,1,0:T(8,128)(2,1)S(1)} async-done(((bf16[32,8,1024]{2,1,0:T(8,128)(2,1)}), bf16[32,8,1024]{2,1,0:T(8,128)(2,1)S(1)}, u32[]{:S(2)}, u32[]{:S(2)}) %all-to-all-start.1) | async-done | bytes 524320 | tf_op jit(solution)/shard_map/all_to_all | solution.py:49
  51.9 8.2 %all-to-all-start.3 = ((bf16[32,8,1024]{2,1,0:T(8,128)(2,1)}), bf16[32,8,1024]{2,1,0:T(8,128)(2,1)S(1)}, u32[]{:S(2)}, u32[]{:S(2)}) async-start(bf16[32,8,1024]{2,1,0:T(8,128)(2,1)} %bitcast.169), calls=%async_computation.3 | async-start | bytes 1048576 | tf_op jit(solution)/shard_map/all_to_all | solution.py:52
  60.3 8.9 %collective-permute-start = (bf16[2,256,128]{2,1,0:T(8,128)(2,1)S(1)}, bf16[2,256,128]{2,1,0:T(8,128)(2,1)S(1)}, u32[]{:S(2)}, u32[]{:S(2)}) collective-permute-start(bf16[2,256,128]{2,1,0:T(8,128)(2,1)S(1)} %pad_maximum_fusion.1), channel_id=1, source_target_pairs={{0,8},{8,16},{16,24},{24,32},{32,40},{40,48},{48,56},{56,64},{64,7... | collective-permute-start | bytes 393224 | tf_op jit(solution)/shard_map/ppermute | solution.py:17
  69.2 1.2 compare_and_fusion
  72.4 4.3 %collective-permute-start.1 = (bf16[2,256,128]{2,1,0:T(8,128)(2,1)S(1)}, bf16[2,256,128]{2,1,0:T(8,128)(2,1)S(1)}, u32[]{:S(2)}, u32[]{:S(2)}) collective-permute-start(bf16[2,256,128]{2,1,0:T(8,128)(2,1)S(1)} %collective-permute-done), channel_id=1, source_target_pairs={{0,8},{8,16},{16,24},{24,32},{32,40},{40,48},{48,56},{56,64},{64,7... | collective-permute-start | bytes 393224 | tf_op jit(solution)/shard_map/ppermute | solution.py:17
  76.7 1.9 %collective-permute-done.1 = bf16[2,256,128]{2,1,0:T(8,128)(2,1)S(1)} collective-permute-done((bf16[2,256,128]{2,1,0:T(8,128)(2,1)S(1)}, bf16[2,256,128]{2,1,0:T(8,128)(2,1)S(1)}, u32[]{:S(2)}, u32[]{:S(2)}) %collective-permute-start.1) | collective-permute-done | bytes 131104 | tf_op jit(solution)/shard_map/ppermute | solution.py:17
  78.8 1.0 conditional.14
  79.8 1.0 conditional.15
  80.8 1.0 conditional.16
  81.8 1.0 conditional.17
  81.9 1.0 convolution_bitcast_fusion
  82.9 1.1 conditional.18
  82.9 1.1 fusion.42
  84.0 5.4 %conditional.19 = (bf16[256,1,8,128]{0,3,2,1:T(8,128)(2,1)}, bf16[256,1024]{1,0:T(8,128)(2,1)S(1)}) conditional(s32[]{:T(128)} %convert_element_type.96, (f32[256,1,8,128]{3,0,2,1:T(8,128)S(1)}) %conditional.18, (pred[256,256]{0,1:T(8,128)(4,1)S(1)}, bf16[256,1,128]{2,0,1:T(8,128)(2,1)S(1)}, bf16[256,1,8,128]{3,2,0,1:T(8,128)(2,1)S(1)}, ...), branch_computations={%region_24.27_spmd, %region_25.28_spmd} | conditional | flops 271056896 | bytes 5447696
  84.0 1.3 %copy.91 = f32[256,1,8,128]{0,3,2,1:T(8,128)} copy(f32[256,1,8,128]{3,0,2,1:T(8,128)S(1)} %get-tuple-element.407) | data formatting | bytes 2097152 | tf_op jit(solution)/shard_map
  85.3 2.8 %fusion.60 = bf16[256,1,8,128]{0,3,2,1:T(8,128)(2,1)} fusion(f32[256,1,8,128]{0,3,2,1:T(8,128)} %copy.91, f32[8,256]{1,0:T(8,128)S(1)} %bitcast.530, pred[256,256]{0,1:T(8,128)(4,1)S(1)} %get-tuple-element.174, bf16[256,1,8,128]{3,2,0,1:T(8,128)(2,1)S(1)} %get-tuple-element.404, bf16[256,1,128]{2,0,1:T(8,128)(2,1)S(1)} %get-tuple-element.406, ...), kind=kOutput, calls=%fused_computation.76 | convolution fusion | flops 271056896 | bytes 2301952 | tf_op jit(solution)/shard_map/cond/branch_1_fun/hgrk,khd->rhgd/dot_general | solution.py:125
  88.1 1.2 %copy.111 = bf16[256,1024]{1,0:T(8,128)(2,1)S(1)} copy(bf16[256,1024]{0,1:T(8,128)(2,1)} %bitcast.63) | data formatting | bytes 1048576 | tf_op jit(solution)/shard_map/conditional
  89.3 0.8 copy-done.1
  90.1 1.4 %copy.92 = bf16[256,1,8,128]{3,2,0,1:T(8,128)(2,1)S(1)} copy(bf16[256,1,8,128]{0,3,2,1:T(8,128)(2,1)} %get-tuple-element.230) | data formatting | bytes 1048576 | tf_op jit(solution)/shard_map/conditional
  91.9 2.7 %conditional.20 = (f32[256,1,8,128]{3,0,2,1:T(8,128)S(1)}, f32[1,256,128]{2,1,0:T(8,128)S(1)}, f32[1,256,128]{2,1,0:T(8,128)S(1)}) conditional(s32[]{:T(128)} %convert_element_type.99, () %tuple.109, (pred[256,256]{0,1:T(8,128)(4,1)S(1)}, bf16[256,1,128]{2,0,1:T(8,128)(2,1)S(1)}, bf16[256,1,8,128]{3,2,0,1:T(8,128)(2,1)S(1)}, ...), branch_computations={%region_27.30_spmd, %region_28.31_spmd} | conditional | flops 675282944 | bytes 13139992 | solution.py:173
  94.6 3.7 %conditional.21 = (f32[256,1,8,128]{3,0,2,1:T(8,128)S(1)}, f32[1,256,128]{2,1,0:T(8,128)}, f32[1,256,128]{2,1,0:T(8,128)S(1)}) conditional(s32[]{:T(128)} %convert_element_type.98, f32[256,1,8,128]{3,0,2,1:T(8,128)S(1)} %get-tuple-element.231, (pred[256,256]{0,1:T(8,128)(4,1)S(1)}, bf16[256,1,128]{2,0,1:T(8,128)(2,1)S(1)}, ...), branch_computations={%region_29.32_spmd, %region_30.33_spmd} | conditional | flops 675545088 | bytes 14450740 | solution.py:173
  94.7 0.6 fusion.95
  96.6 1.1 convolution_bitcast_fusion.8
  97.7 0.6 fusion.97
  98.3 4.0 %conditional.22 = (f32[256,1,8,128]{3,0,2,1:T(8,128)S(1)}, f32[1,256,128]{2,1,0:T(8,128)}, f32[1,256,128]{2,1,0:T(8,128)}) conditional(s32[]{:T(128)} %convert_element_type.96, f32[256,1,8,128]{3,0,2,1:T(8,128)S(1)} %get-tuple-element.232, (pred[256,256]{0,1:T(8,128)(4,1)S(1)}, bf16[256,1,128]{2,0,1:T(8,128)(2,1)S(1)}, ...), branch_computations={%region_31.34_spmd, %region_32.35_spmd} | conditional | flops 675545088 | bytes 14188568 | solution.py:173
  98.4 0.6 fusion.114
  99.0 1.1 convolution_bitcast_fusion.10
  100.6 1.1 convolution_bitcast_fusion.11
  101.7 0.6 fusion.116
  102.3 1.0 pad_maximum_fusion
  103.3 1.9 %collective-permute-start.2 = (f32[2,256,128]{2,1,0:T(8,128)S(1)}, f32[2,256,128]{2,1,0:T(8,128)S(1)}, u32[]{:S(2)}, u32[]{:S(2)}) collective-permute-start(f32[2,256,128]{2,1,0:T(8,128)S(1)} %pad_maximum_fusion), channel_id=1, source_target_pairs={{8,0},{16,8},{24,16},{32,24},{40,32},{48,40},{56,48},{64,56},{72,6... | collective-permute-start | bytes 786440 | tf_op jit(solution)/shard_map/ppermute | solution.py:17
  105.2 7.0 %collective-permute-done.2 = f32[2,256,128]{2,1,0:T(8,128)S(1)} collective-permute-done((f32[2,256,128]{2,1,0:T(8,128)S(1)}, f32[2,256,128]{2,1,0:T(8,128)S(1)}, u32[]{:S(2)}, u32[]{:S(2)}) %collective-permute-start.2) | collective-permute-done | bytes 262176 | tf_op jit(solution)/shard_map/ppermute | solution.py:17
  112.2 0.9 maximum_add_fusion
  113.2 1.9 %collective-permute-start.3 = (f32[2,256,128]{2,1,0:T(8,128)S(1)}, f32[2,256,128]{2,1,0:T(8,128)S(1)}, u32[]{:S(2)}, u32[]{:S(2)}) collective-permute-start(f32[2,256,128]{2,1,0:T(8,128)S(1)} %maximum_add_fusion), channel_id=1, source_target_pairs={{8,0},{16,8},{24,16},{32,24},{40,32},{48,40},{56,48},{64,56},{72,6... | collective-permute-start | bytes 786440 | tf_op jit(solution)/shard_map/ppermute | solution.py:17
  115.5 0.9 copy.198
  116.4 5.6 %collective-permute-done.3 = f32[2,256,128]{2,1,0:T(8,128)S(1)} collective-permute-done((f32[2,256,128]{2,1,0:T(8,128)S(1)}, f32[2,256,128]{2,1,0:T(8,128)S(1)}, u32[]{:S(2)}, u32[]{:S(2)}) %collective-permute-start.3) | collective-permute-done | bytes 262176 | tf_op jit(solution)/shard_map/ppermute | solution.py:17
  122.1 0.7 slice_bitcast_fusion
  (60 shorter events, 9.9 us)
Async XLA Ops:
  0.6 14.1 %copy-start = (bf16[32,8192]{1,0:T(8,128)(2,1)S(1)}, bf16[32,8192]{1,0:T(8,128)(2,1)}, u32[]{:S(2)}) copy-start(bf16[32,8192]{1,0:T(8,128)(2,1)} %param.31) | copy-start | bytes 1572868
  0.6 14.7 %copy-start.2 = (bf16[32,8192]{1,0:T(8,128)(2,1)S(1)}, bf16[32,8192]{1,0:T(8,128)(2,1)}, u32[]{:S(2)}) copy-start(bf16[32,8192]{1,0:T(8,128)(2,1)} %param.28) | copy-start | bytes 1572868
  5.3 15.5 %all-to-all-start = ((bf16[32,8,128]{2,1,0:T(8,128)(2,1)}), bf16[32,8,128]{2,1,0:T(8,128)(2,1)S(1)}, u32[]{:S(2)}, u32[]{:S(2)}) async-start(bf16[32,8,128]{2,1,0:T(8,128)(2,1)} %bitcast.149), calls=%async_computation | async-start | bytes 131072 | tf_op jit(solution)/shard_map/all_to_all | solution.py:50
  20.8 12.7 %all-to-all-start.2 = ((bf16[32,8,128]{2,1,0:T(8,128)(2,1)}), bf16[32,8,128]{2,1,0:T(8,128)(2,1)S(1)}, u32[]{:S(2)}, u32[]{:S(2)}) async-start(bf16[32,8,128]{2,1,0:T(8,128)(2,1)} %bitcast.159), calls=%async_computation.2 | async-start | bytes 131072 | tf_op jit(solution)/shard_map/all_to_all | solution.py:51
  33.5 18.4 %all-to-all-start.1 = ((bf16[32,8,1024]{2,1,0:T(8,128)(2,1)}), bf16[32,8,1024]{2,1,0:T(8,128)(2,1)S(1)}, u32[]{:S(2)}, u32[]{:S(2)}) async-start(bf16[32,8,1024]{2,1,0:T(8,128)(2,1)} %bitcast.154), calls=%async_computation.1 | async-start | bytes 1048576 | tf_op jit(solution)/shard_map/all_to_all | solution.py:49
  51.9 26.8 %all-to-all-start.3 = ((bf16[32,8,1024]{2,1,0:T(8,128)(2,1)}), bf16[32,8,1024]{2,1,0:T(8,128)(2,1)S(1)}, u32[]{:S(2)}, u32[]{:S(2)}) async-start(bf16[32,8,1024]{2,1,0:T(8,128)(2,1)} %bitcast.169), calls=%async_computation.3 | async-start | bytes 1048576 | tf_op jit(solution)/shard_map/all_to_all | solution.py:52
  60.3 12.1 %collective-permute-start = (bf16[2,256,128]{2,1,0:T(8,128)(2,1)S(1)}, bf16[2,256,128]{2,1,0:T(8,128)(2,1)S(1)}, u32[]{:S(2)}, u32[]{:S(2)}) collective-permute-start(bf16[2,256,128]{2,1,0:T(8,128)(2,1)S(1)} %pad_maximum_fusion.1), channel_id=1, source_target_pairs={{0,8},{8,16},{16,24},{24,32},{32,40},{40,48},{48,56},{56,64},{64,7... | collective-permute-start | bytes 393224 | tf_op jit(solution)/shard_map/ppermute | solution.py:17
  72.4 6.2 %collective-permute-start.1 = (bf16[2,256,128]{2,1,0:T(8,128)(2,1)S(1)}, bf16[2,256,128]{2,1,0:T(8,128)(2,1)S(1)}, u32[]{:S(2)}, u32[]{:S(2)}) collective-permute-start(bf16[2,256,128]{2,1,0:T(8,128)(2,1)S(1)} %collective-permute-done), channel_id=1, source_target_pairs={{0,8},{8,16},{16,24},{24,32},{32,40},{40,48},{48,56},{56,64},{64,7... | collective-permute-start | bytes 393224 | tf_op jit(solution)/shard_map/ppermute | solution.py:17
  76.7 6.1 %copy-start.3 = (bf16[256,1,128]{2,0,1:T(8,128)(2,1)}, bf16[256,1,128]{2,0,1:T(8,128)(2,1)S(1)}, u32[]{:S(2)}) copy-start(bf16[256,1,128]{2,0,1:T(8,128)(2,1)S(1)} %get-tuple-element.458) | copy-start | bytes 196612
  89.3 0.8 copy-start.1
  95.3 0.8 copy-start.4
  103.3 8.9 %collective-permute-start.2 = (f32[2,256,128]{2,1,0:T(8,128)S(1)}, f32[2,256,128]{2,1,0:T(8,128)S(1)}, u32[]{:S(2)}, u32[]{:S(2)}) collective-permute-start(f32[2,256,128]{2,1,0:T(8,128)S(1)} %pad_maximum_fusion), channel_id=1, source_target_pairs={{8,0},{16,8},{24,16},{32,24},{40,32},{48,40},{56,48},{64,56},{72,6... | collective-permute-start | bytes 786440 | tf_op jit(solution)/shard_map/ppermute | solution.py:17
  113.2 8.9 %collective-permute-start.3 = (f32[2,256,128]{2,1,0:T(8,128)S(1)}, f32[2,256,128]{2,1,0:T(8,128)S(1)}, u32[]{:S(2)}, u32[]{:S(2)}) collective-permute-start(f32[2,256,128]{2,1,0:T(8,128)S(1)} %maximum_add_fusion), channel_id=1, source_target_pairs={{8,0},{16,8},{24,16},{32,24},{40,32},{48,40},{56,48},{64,56},{72,6... | collective-permute-start | bytes 786440 | tf_op jit(solution)/shard_map/ppermute | solution.py:17
where the time goes:
time: 124 us; the launch traced here: 123 us
  starting transfers between devices  48.2 us (39%)
  waiting for transfers between devices  34.9 us (28%)
  matrix products  15.8 us (13%)
  local copies, waits for them, and re-layouts  12.4 us (10%)
  other arithmetic  7.99 us (6%)
  between operations  2.95 us (2%)
    ppermute x4, starting transfers between devices, shifted(): return lax.ppermute(x, axis, pairs)  17.1 us
    ppermute x4, waiting for transfers between devices, shifted(): return lax.ppermute(x, axis, pairs)  14.5 us
    all_to_all x1, waiting for transfers between devices, on_device(): lax.all_to_all(spread(q_dealt), ('dp', 'tensor'), split_axis=0, concat_ax...  10.7 us
    all_to_all x1, starting transfers between devices, on_device(): lax.all_to_all(spread(k_dealt), ('dp', 'tensor'), split_axis=0, concat_ax...  9.44 us
    all_to_all x1, starting transfers between devices, on_device(): lax.all_to_all(spread(g_dealt), ('dp', 'tensor'), split_axis=0, concat_ax...  8.21 us
    all_to_all x1, starting transfers between devices, on_device(): lax.all_to_all(spread(q_dealt), ('dp', 'tensor'), split_axis=0, concat_ax...  6.74 us
    all_to_all x1, starting transfers between devices, on_device(): lax.all_to_all(spread(v_dealt), ('dp', 'tensor'), split_axis=0, concat_ax...  6.7 us
    all_to_all x1, waiting for transfers between devices, on_device(): lax.all_to_all(spread(v_dealt), ('dp', 'tensor'), split_axis=0, concat_ax...  4.89 us
  transfers between devices with their start and end apart: 8, of which 6 were waited for; matrix products, arithmetic and copies ran while one was open for 5% of the time, Pallas kernels for 0%

commit v1 on v0

v1 whole, which is shorter than its diff:
```python
import functools

import jax
import jax.numpy as jnp
from jax import lax
from jax.experimental import pallas as pl
from jax.experimental.pallas import tpu as pltpu
from jax.sharding import PartitionSpec as P

HEAD = 128
QUERY_GROUP = 8
NEARBY = 3
MESH = pl.DeviceIdType.MESH
MASKED = -1e30
SCALE = HEAD ** (-0.5)
LOG2E = 1.4426950408889634

NT = (((1,), (1,)), ((), ()))
NN = (((1,), (0,)), ((), ()))


def dot(a, b, dims):
    return lax.dot_general(a, b, dims, preferred_element_type=jnp.float32)


def kernel(
    n_dp, n_ctx, n_lane, sub,
    q_hbm, k_hbm, v_hbm, g_hbm, lengths, plan_hbm,
    out_hbm, dq_hbm, dk_ref, dv_ref,
    q_in, k_in, v_in, g_in, plan,
    q_send, kv_send, g_send, q_rows, kv_rows, g_rows,
    bias, probs, kt, vt, gt, delta, dqt, part_send, part_recv, dkv_acc, out_buf, dq_buf,
    in_sem, plan_sem, q_sems, kv_sems, g_sems, halo_send, halo_recv, back_send, back_recv, out_sem,
):
    s = lax.axis_index("dp")
    c = lax.axis_index("context")
    t = lax.axis_index("tensor")
    peers = n_dp * n_lane
    me = s * n_lane + t
    tok = peers * sub
    width = QUERY_GROUP * HEAD

    def ctx(by):
        return {"context": lax.rem(c + by + n_ctx, n_ctx)}

    def peer(i):
        r = lax.rem(s + i // n_lane, n_dp)
        lane = lax.rem(t + lax.rem(i, n_lane), n_lane)
        return r, lane

    barrier = pltpu.get_barrier_semaphore()

    def greet(i, carry):
        r, lane = peer(i)
        pl.semaphore_signal(
            barrier, inc=1, device_id={"dp": r, "tensor": lane}, device_id_type=MESH
        )
        return carry

    lax.fori_loop(1, peers, greet, 0)
    for by in (-2, -1, 1, 2):
        pl.semaphore_signal(barrier, inc=1, device_id=ctx(by), device_id_type=MESH)

    plan_copy = pltpu.make_async_copy(plan_hbm.at[s], plan, plan_sem)
    plan_copy.start()
    loads = [
        pltpu.make_async_copy(a, b, in_sem.at[n])
        for n, (a, b) in enumerate(
            ((k_hbm, k_in), (v_hbm, v_in), (q_hbm, q_in), (g_hbm, g_in))
        )
    ]
    for copy in loads:
        copy.start()
    plan_copy.wait()
    for copy in loads:
        copy.wait()

    for r in range(n_dp):
        block = jnp.int32(0)
        for b in range(n_dp):
            block = jnp.where(plan[t, b, c] == r, jnp.int32(b), block)
        k_block = k_in[block]
        v_block = v_in[block]
        for lane in range(n_lane):
            kv_send[r * n_lane + lane, :, 0:HEAD] = k_block[:, lane * HEAD : (lane + 1) * HEAD]
            kv_send[r * n_lane + lane, :, HEAD:] = v_block[:, lane * HEAD : (lane + 1) * HEAD]
        q_block = q_in[block]
        g_block = g_in[block]
        for lane in range(n_lane):
            q_send[r * n_lane + lane] = q_block[:, lane * width : (lane + 1) * width]
            g_send[r * n_lane + lane] = g_block[:, lane * width : (lane + 1) * width]

    p = c * tok + lax.broadcasted_iota(jnp.int32, (1, tok), 1)

    def next_bound(n, carry):
        bound, start = carry
        bound = bound + lengths[s, n]
        return bound, jnp.maximum(start, jnp.where(bound <= p, bound, 0))

    _, start = lax.fori_loop(
        0, lengths.shape[1], next_bound, (jnp.int32(0), jnp.zeros((1, tok), jnp.int32))
    )
    j = (c - (NEARBY - 1)) * tok + lax.broadcasted_iota(jnp.int32, (NEARBY * tok, 1), 0)
    bias[...] = jnp.where((j <= p) & (j >= start), 0.0, MASKED).astype(jnp.float32)

    pl.semaphore_wait(barrier, peers - 1 + 4)

    own = (NEARBY - 1) * tok

    def my_rows(base):
        return pl.ds(pl.multiple_of(base + me * sub, sub), sub)

    def deal(sent, rows, base, sems):
        def one(i, carry):
            r, lane = peer(i)
            pltpu.make_async_remote_copy(
                src_ref=sent.at[r * n_lane + lane],
                dst_ref=rows.at[my_rows(base)],
                send_sem=sems.at[0],
                recv_sem=sems.at[1],
                device_id={"dp": r, "tensor": lane},
                device_id_type=MESH,
            ).start()
            return carry

        lax.fori_loop(1, peers, one, 0)
        pltpu.make_async_copy(sent.at[me], rows.at[my_rows(base)], sems.at[1]).start()

    deal(kv_send, kv_rows, own, kv_sems)
    deal(q_send, q_rows, 0, q_sems)
    deal(g_send, g_rows, 0, g_sems)

    def arrived(rows, sems):
        pltpu.make_async_copy(rows, rows, sems.at[1]).wait()

    own_kv = kv_rows.at[pl.ds(own, tok)]
    arrived(own_kv, kv_sems)
    halo = []
    for d in range(1, NEARBY):
        copy = pltpu.make_async_remote_copy(
            src_ref=own_kv,
            dst_ref=kv_rows.at[pl.ds(own - d * tok, tok)],
            send_sem=halo_send.at[d - 1],
            recv_sem=halo_recv.at[d - 1],
            device_id=ctx(d),
            device_id_type=MESH,
        )
        copy.start()
        halo.append(copy)
    for copy in halo:
        copy.wait()
    kt[...] = kv_rows[:, 0:HEAD].astype(jnp.float32).T.astype(jnp.bfloat16)
    vt[...] = kv_rows[:, HEAD:].astype(jnp.float32).T.astype(jnp.bfloat16)

    arrived(q_rows, q_sems)

    def head(h):
        return pl.ds(pl.multiple_of(h * HEAD, HEAD), HEAD)

    def forward(h, carry):
        scores = dot(kv_rows[:, 0:HEAD], q_rows[:, head(h)], NT) * (SCALE * LOG2E) + bias[...]
        top = jnp.max(scores, axis=0, keepdims=True)
        e = jnp.exp2(scores - top)
        pr = e * (1.0 / jnp.sum(e, axis=0, keepdims=True))
        probs[h] = pr
        o = dot(vt[...], pr.astype(jnp.bfloat16), NN)
        out_buf[:, head(h)] = o.T.astype(jnp.bfloat16)
        return carry

    lax.fori_loop(0, QUERY_GROUP, forward, 0)
    out_copy = pltpu.make_async_copy(out_buf, out_hbm, out_sem.at[0])
    out_copy.start()

    arrived(g_rows, g_sems)

    def turn(h, carry):
        g_f = g_rows[:, head(h)].astype(jnp.float32).T
        o_t = out_buf[:, head(h)].astype(jnp.float32).T
        gt[h] = g_f.astype(jnp.bfloat16)
        delta[h] = jnp.sum(g_f * o_t, axis=0, keepdims=True)
        return carry

    lax.fori_loop(0, QUERY_GROUP, turn, 0)

    def backward(n, h):
        at = pl.ds(n * tok, tok)
        pr = probs[h, at]
        dprob = dot(kv_rows[at, HEAD:], gt[h], NN)
        ds = (SCALE * pr * (dprob - delta[h])).astype(jnp.bfloat16)
        term = dot(kt[:, at], ds, NN)
        dqt[h] = term if n == 0 else dqt[h] + term
        dk = dot(ds, q_rows[:, head(h)], NN)
        dv = dot(pr.astype(jnp.bfloat16), g_rows[:, head(h)], NN)
        return dk, dv

    back = []

    def send_part(n):
        copy = pltpu.make_async_remote_copy(
            src_ref=part_send.at[n],
            dst_ref=part_recv.at[n],
            send_sem=back_send.at[n],
            recv_sem=back_recv.at[n],
            device_id=ctx(n - (NEARBY - 1)),
            device_id_type=MESH,
        )
        copy.start()
        back.append(copy)

    for n in range(NEARBY):
        dk, dv = backward(n, 0)
        dkv_acc[:, 0:HEAD] = dk
        dkv_acc[:, HEAD:] = dv
        if n > 0:
            send_part(n - 1)

        def more(h, carry, n=n):
            dk, dv = backward(n, h)
            dkv_acc[:, 0:HEAD] += dk
            dkv_acc[:, HEAD:] += dv
            if n == NEARBY - 1:
                dq_buf[:, head(h)] = dqt[h].T.astype(jnp.bfloat16)
            return carry

        lax.fori_loop(1, QUERY_GROUP, more, 0)
        if n == NEARBY - 1:
            dq_buf[:, 0:HEAD] = dqt[0].T.astype(jnp.bfloat16)
        else:
            part_send[n] = dkv_acc[...].astype(jnp.bfloat16)

    dq_copy = pltpu.make_async_copy(dq_buf, dq_hbm, out_sem.at[1])
    dq_copy.start()
    for copy in back:
        copy.wait()
    total = dkv_acc[...]
    for n in range(NEARBY - 1):
        total = total + part_recv[n].astype(jnp.float32)
    dk_ref[...] = total[:, 0:HEAD].astype(jnp.bfloat16)
    dv_ref[...] = total[:, HEAD:].astype(jnp.bfloat16)

    for sent, sems in ((kv_send, kv_sems), (q_send, q_sems), (g_send, g_sems)):
        gone = sent.at[pl.ds(0, peers - 1)]
        pltpu.make_async_copy(gone, gone, sems.at[0]).wait()
    out_copy.wait()
    dq_copy.wait()


def solution(mesh):
    n_dp, n_ctx, n_lane = (mesh.shape[a] for a in ("dp", "context", "tensor"))

    def on_device(queries, keys, values, grad_out, doc_lengths, deal_plan):
        rows = queries.shape[0]
        sub = rows // n_dp
        peers = n_dp * n_lane
        tok = peers * sub
        width = QUERY_GROUP * HEAD
        bf, f32 = jnp.bfloat16, jnp.float32
        split = [a.reshape(n_dp, sub, a.shape[1]) for a in (queries, keys, values, grad_out)]
        any_ = pl.BlockSpec(memory_space=pl.ANY)
        vmem = pl.BlockSpec(memory_space=pltpu.VMEM)
        smem = pl.BlockSpec(memory_space=pltpu.SMEM)
        dma = pltpu.SemaphoreType.DMA
        return pl.pallas_call(
            functools.partial(kernel, n_dp, n_ctx, n_lane, sub),
            out_shape=(
                jax.ShapeDtypeStruct((tok, width), bf),
                jax.ShapeDtypeStruct((tok, width), bf),
                jax.ShapeDtypeStruct((tok, HEAD), bf),
                jax.ShapeDtypeStruct((tok, HEAD), bf),
            ),
            in_specs=[any_, any_, any_, any_, smem, any_],
            out_specs=(any_, any_, vmem, vmem),
            scratch_shapes=[
                pltpu.VMEM((n_dp, sub, n_lane * width), bf),
                pltpu.VMEM((n_dp, sub, n_lane * HEAD), bf),
                pltpu.VMEM((n_dp, sub, n_lane * HEAD), bf),
                pltpu.VMEM((n_dp, sub, n_lane * width), bf),
                pltpu.SMEM((n_lane, n_dp, n_ctx), jnp.int32),
                pltpu.VMEM((peers, sub, width), bf),
                pltpu.VMEM((peers, sub, 2 * HEAD), bf),
                pltpu.VMEM((peers, sub, width), bf),
                pltpu.VMEM((tok, width), bf),
                pltpu.VMEM((NEARBY * tok, 2 * HEAD), bf),
                pltpu.VMEM((tok, width), bf),
                pltpu.VMEM((NEARBY * tok, tok), f32),
                pltpu.VMEM((QUERY_GROUP, NEARBY * tok, tok), f32),
                pltpu.VMEM((HEAD, NEARBY * tok), bf),
                pltpu.VMEM((HEAD, NEARBY * tok), bf),
                pltpu.VMEM((QUERY_GROUP, HEAD, tok), bf),
                pltpu.VMEM((QUERY_GROUP, 1, tok), f32),
                pltpu.VMEM((QUERY_GROUP, HEAD, tok), f32),
                pltpu.VMEM((NEARBY - 1, tok, 2 * HEAD), bf),
                pltpu.VMEM((NEARBY - 1, tok, 2 * HEAD), bf),
                pltpu.VMEM((tok, 2 * HEAD), f32),
                pltpu.VMEM((tok, width), bf),
                pltpu.VMEM((tok, width), bf),
                dma((4,)),
                dma,
                dma((2,)),
                dma((2,)),
                dma((2,)),
                dma((NEARBY - 1,)),
                dma((NEARBY - 1,)),
                dma((NEARBY - 1,)),
                dma((NEARBY - 1,)),
                dma((2,)),
            ],
            compiler_params=pltpu.CompilerParams(
                collective_id=0, has_side_effects=True, vmem_limit_bytes=48 * 1024 * 1024
            ),
        )(*split, doc_lengths, deal_plan.transpose(1, 2, 3, 0))

    arriving = P(("dp", "context", "tensor"), None)
    leaving = P(("dp", "context"), "tensor")
    return jax.shard_map(
        on_device,
        mesh=mesh,
        in_specs=(arriving, arriving, arriving, arriving, P(), P()),
        out_specs=(leaving, leaving, leaving, leaving),
        check_vma=False,
    )
```

time: 124 us -> 64.3 us (0.52)
  the two profiles are of different devices: /device:TPU:213 before, /device:TPU:2 now
where the time goes in v1:
time: 64.3 us; the launch traced here: 63.9 us
  Pallas kernels  55.2 us (86%)
  local copies, waits for them, and re-layouts  8.12 us (13%)
  between operations  0.66 us (1%)
    pallas_call x1, Pallas kernels, on_device(): pl.pallas_call(functools.partial(kernel, n_dp, n_ctx, n_lane, sub), out_s...  55.2 us
    unnamed x16, local copies, waits for them, and re-layouts  8.12 us

profile of v1, /device:TPU:2, one launch (start us, length us, event | category | flops | bytes accessed | tf_op | source)
XLA Modules:
  0.0 63.9 jit_solution(1691497480291680384)
XLA Ops:
  0.6 0.0 copy-start.5
  0.6 0.7 %copy-done.5 = s32[4,32]{1,0:T(4,128)S(1)} copy-done((s32[4,32]{1,0:T(4,128)S(1)}, s32[4,32]{1,0:T(4,128)}, u32[]{:S(2)}) %copy-start.5) | copy-done | bytes 536
  1.3 0.0 copy-start
  1.3 1.0 %copy-done = bf16[32,8192]{1,0:T(8,128)(2,1)S(1)} copy-done((bf16[32,8192]{1,0:T(8,128)(2,1)S(1)}, bf16[32,8192]{1,0:T(8,128)(2,1)}, u32[]{:S(2)}) %copy-start) | copy-done | bytes 524312
  2.4 0.0 copy-start.1
  2.4 1.0 %copy-done.1 = bf16[32,8192]{1,0:T(8,128)(2,1)S(1)} copy-done((bf16[32,8192]{1,0:T(8,128)(2,1)S(1)}, bf16[32,8192]{1,0:T(8,128)(2,1)}, u32[]{:S(2)}) %copy-start.1) | copy-done | bytes 524312
  3.4 0.0 copy-start.2
  3.4 0.8 %copy-done.2 = bf16[32,1024]{1,0:T(8,128)(2,1)S(1)} copy-done((bf16[32,1024]{1,0:T(8,128)(2,1)S(1)}, bf16[32,1024]{1,0:T(8,128)(2,1)}, u32[]{:S(2)}) %copy-start.2) | copy-done | bytes 65560
  4.2 0.0 copy-start.3
  4.2 0.8 %copy-done.3 = bf16[32,1024]{1,0:T(8,128)(2,1)S(1)} copy-done((bf16[32,1024]{1,0:T(8,128)(2,1)S(1)}, bf16[32,1024]{1,0:T(8,128)(2,1)}, u32[]{:S(2)}) %copy-start.3) | copy-done | bytes 65560
  5.1 0.0 copy-start.4
  5.1 0.8 %copy-done.4 = s32[16,4,8,4]{0,3,2,1:T(4,128)S(1)} copy-done((s32[16,4,8,4]{0,3,2,1:T(4,128)S(1)}, s32[16,4,8,4]{0,3,2,1:T(4,128)}, u32[]{:S(2)}) %copy-start.4) | copy-done | bytes 8216
  5.9 55.2 %shard_map.93 = (bf16[256,1024]{1,0:T(8,128)(2,1)S(1)}, bf16[256,1024]{1,0:T(8,128)(2,1)S(1)}, bf16[256,128]{1,0:T(8,128)(2,1)S(1)}, bf16[256,128]{1,0:T(8,128)(2,1)S(1)}) custom-call(bf16[4,8,8192]{2,1,0:T(8,128)(2,1)S(1)} %bitcast.5, bf16[4,8,1024]{2,1,0:T(8,128)(2,1)S(1)} %bitcast.7, bf16[4,8,1024]{2,1,0:T(8,128)(2,1)S(1)} %bitcast.8, ...), custom_call_target="tpu_custom_call" | custom-call | tf_op jit(solution)/shard_map/pallas_call | solution.py:263
  61.1 0.8 %copy.14 = bf16[256,1024]{1,0:T(8,128)(2,1)} copy(bf16[256,1024]{1,0:T(8,128)(2,1)S(1)} %get-tuple-element.8) | data formatting | bytes 1048576
  61.9 0.8 %copy.15 = bf16[256,1024]{1,0:T(8,128)(2,1)} copy(bf16[256,1024]{1,0:T(8,128)(2,1)S(1)} %get-tuple-element.9) | data formatting | bytes 1048576
  62.7 0.6 copy.16
  63.3 0.6 copy.17
Async XLA Ops:
  0.6 0.7 %copy-start.5 = (s32[4,32]{1,0:T(4,128)S(1)}, s32[4,32]{1,0:T(4,128)}, u32[]{:S(2)}) copy-start(s32[4,32]{1,0:T(4,128)} %lengths.1) | copy-start | bytes 1540
  1.3 1.0 %copy-start = (bf16[32,8192]{1,0:T(8,128)(2,1)S(1)}, bf16[32,8192]{1,0:T(8,128)(2,1)}, u32[]{:S(2)}) copy-start(bf16[32,8192]{1,0:T(8,128)(2,1)} %param.6) | copy-start | bytes 1572868
  2.4 1.0 %copy-start.1 = (bf16[32,8192]{1,0:T(8,128)(2,1)S(1)}, bf16[32,8192]{1,0:T(8,128)(2,1)}, u32[]{:S(2)}) copy-start(bf16[32,8192]{1,0:T(8,128)(2,1)} %param.9) | copy-start | bytes 1572868
  3.4 0.8 %copy-start.2 = (bf16[32,1024]{1,0:T(8,128)(2,1)S(1)}, bf16[32,1024]{1,0:T(8,128)(2,1)}, u32[]{:S(2)}) copy-start(bf16[32,1024]{1,0:T(8,128)(2,1)} %param.7) | copy-start | bytes 196612
  4.2 0.8 %copy-start.3 = (bf16[32,1024]{1,0:T(8,128)(2,1)S(1)}, bf16[32,1024]{1,0:T(8,128)(2,1)}, u32[]{:S(2)}) copy-start(bf16[32,1024]{1,0:T(8,128)(2,1)} %param.8) | copy-start | bytes 196612
  5.1 0.8 %copy-start.4 = (s32[16,4,8,4]{0,3,2,1:T(4,128)S(1)}, s32[16,4,8,4]{0,3,2,1:T(4,128)}, u32[]{:S(2)}) copy-start(s32[16,4,8,4]{0,3,2,1:T(4,128)} %param.11) | copy-start | bytes 24580

commit v2 on v1

--- a/solution.py
+++ b/solution.py
@@ -245,6 +245,15 @@
     dq_copy.wait()
 
 
+def store(*refs):
+    sems = refs[8]
+    copies = [pltpu.make_async_copy(refs[n], refs[n + 4], sems.at[n]) for n in range(4)]
+    for copy in copies:
+        copy.start()
+    for copy in copies:
+        copy.wait()
+
+
 def solution(mesh):
     n_dp, n_ctx, n_lane = (mesh.shape[a] for a in ("dp", "context", "tensor"))
 
@@ -255,20 +264,25 @@
         tok = peers * sub
         width = QUERY_GROUP * HEAD
         bf, f32 = jnp.bfloat16, jnp.float32
-        split = [a.reshape(n_dp, sub, a.shape[1]) for a in (queries, keys, values, grad_out)]
+        split = [
+            pltpu.with_memory_space_constraint(a.reshape(n_dp, sub, a.shape[1]), pltpu.HBM)
+            for a in (queries, keys, values, grad_out)
+        ]
+        plans = pltpu.with_memory_space_constraint(deal_plan.transpose(1, 2, 3, 0), pltpu.HBM)
         any_ = pl.BlockSpec(memory_space=pl.ANY)
+        hbm = pl.BlockSpec(memory_space=pltpu.HBM)
         vmem = pl.BlockSpec(memory_space=pltpu.VMEM)
         smem = pl.BlockSpec(memory_space=pltpu.SMEM)
         dma = pltpu.SemaphoreType.DMA
-        return pl.pallas_call(
+        results = pl.pallas_call(
             functools.partial(kernel, n_dp, n_ctx, n_lane, sub),
             out_shape=(
-                jax.ShapeDtypeStruct((tok, width), bf),
-                jax.ShapeDtypeStruct((tok, width), bf),
-                jax.ShapeDtypeStruct((tok, HEAD), bf),
-                jax.ShapeDtypeStruct((tok, HEAD), bf),
+                pltpu.VMEM((tok, width), bf),
+                pltpu.VMEM((tok, width), bf),
+                pltpu.VMEM((tok, HEAD), bf),
+                pltpu.VMEM((tok, HEAD), bf),
             ),
-            in_specs=[any_, any_, any_, any_, smem, any_],
+            in_specs=[hbm, hbm, hbm, hbm, smem, hbm],
             out_specs=(any_, any_, vmem, vmem),
             scratch_shapes=[
                 pltpu.VMEM((n_dp, sub, n_lane * width), bf),
@@ -308,7 +322,14 @@
             compiler_params=pltpu.CompilerParams(
                 collective_id=0, has_side_effects=True, vmem_limit_bytes=48 * 1024 * 1024
             ),
-        )(*split, doc_lengths, deal_plan.transpose(1, 2, 3, 0))
+        )(*split, doc_lengths, plans)
+        return pl.pallas_call(
+            store,
+            out_shape=tuple(pltpu.HBM(a.shape, a.dtype) for a in results),
+            in_specs=[vmem] * 4,
+            out_specs=(hbm,) * 4,
+            scratch_shapes=[dma((4,))],
+        )(*[pltpu.with_memory_space_constraint(a, pltpu.VMEM) for a in results])
 
     arriving = P(("dp", "context", "tensor"), None)
     leaving = P(("dp", "context"), "tensor")

time: 64.3 us -> 57.7 us (0.90)
  local copies, waits for them, and re-layouts: 8.12 us -> 0.67 us
  Pallas kernels: 55.2 us -> 56.2 us
    unnamed x16 -> x2, local copies, waits for them, and re-layouts: 8.12 us -> 0.67 us
    pallas_call x0 -> x1, Pallas kernels: none -> 1.03 us  [on_device(): pl.pallas_call(store, out_shape=tuple((pltpu.HBM(a.shape, a.dtype) for a...]
where the time goes in v2:
time: 57.7 us; the launch traced here: 57.5 us
  Pallas kernels  56.2 us (97%)
  local copies, waits for them, and re-layouts  0.67 us (1%)
  between operations  0.65 us (1%)
    pallas_call x1, Pallas kernels, on_device(): pl.pallas_call(functools.partial(kernel, n_dp, n_ctx, n_lane, sub), out_s...  55.2 us

profile of v2, /device:TPU:2, one launch (start us, length us, event | category | flops | bytes accessed | tf_op | source)
XLA Modules:
  0.0 57.5 jit_solution(14017771504230616879)
XLA Ops:
  0.6 0.0 copy-start
  0.6 0.7 %copy-done = s32[4,32]{1,0:T(4,128)S(1)} copy-done((s32[4,32]{1,0:T(4,128)S(1)}, s32[4,32]{1,0:T(4,128)}, u32[]{:S(2)}) %copy-start) | copy-done | bytes 536
  1.3 55.2 %shard_map.93 = (bf16[256,1024]{1,0:T(8,128)(2,1)S(1)}, bf16[256,1024]{1,0:T(8,128)(2,1)S(1)}, bf16[256,128]{1,0:T(8,128)(2,1)S(1)}, bf16[256,128]{1,0:T(8,128)(2,1)S(1)}) custom-call(bf16[4,8,8192]{2,1,0:T(8,128)(2,1)} %bitcast.5, bf16[4,8,1024]{2,1,0:T(8,128)(2,1)} %bitcast.7, bf16[4,8,1024]{2,1,0:T(8,128)(2,1)} %bitcast.8, bf16[4,8,8192]{2,1,0:T(8,128)(2,1)} %bitcast.6, ...), custom_call_target="tpu_custom_call" | custom-call | tf_op jit(solution)/shard_map/pallas_call | solution.py:277
  56.5 1.0 %shard_map.94 = (bf16[256,1024]{1,0:T(8,128)(2,1)}, bf16[256,1024]{1,0:T(8,128)(2,1)}, bf16[256,128]{1,0:T(8,128)(2,1)}, bf16[256,128]{1,0:T(8,128)(2,1)}) custom-call(bf16[256,1024]{1,0:T(8,128)(2,1)S(1)} %get-tuple-element.8.refs_0_, bf16[256,1024]{1,0:T(8,128)(2,1)S(1)} %get-tuple-element.9.refs_1_, bf16[256,128]{1,0:T(8,128)(2,1)S(1)} %get-tuple-element.10.refs_2_, ...), custom_call_target="tpu_custom_call" | custom-call | tf_op jit(solution)/shard_map/pallas_call | solution.py:326
Async XLA Ops:
  0.6 0.7 %copy-start = (s32[4,32]{1,0:T(4,128)S(1)}, s32[4,32]{1,0:T(4,128)}, u32[]{:S(2)}) copy-start(s32[4,32]{1,0:T(4,128)} %lengths.1) | copy-start | bytes 1540

commit v3 on v2

--- a/solution.py
+++ b/solution.py
@@ -11,6 +11,7 @@
 QUERY_GROUP = 8
 NEARBY = 3
 MESH = pl.DeviceIdType.MESH
+GROUPS = ((0, 4), (4, 6), (6, 8))
 MASKED = -1e30
 SCALE = HEAD ** (-0.5)
 LOG2E = 1.4426950408889634
@@ -110,12 +111,12 @@
     def my_rows(base):
         return pl.ds(pl.multiple_of(base + me * sub, sub), sub)
 
-    def deal(sent, rows, base, sems):
+    def deal(sent, rows, base, sems, cols):
         def one(i, carry):
             r, lane = peer(i)
             pltpu.make_async_remote_copy(
-                src_ref=sent.at[r * n_lane + lane],
-                dst_ref=rows.at[my_rows(base)],
+                src_ref=sent.at[r * n_lane + lane, :, cols],
+                dst_ref=rows.at[my_rows(base), cols],
                 send_sem=sems.at[0],
                 recv_sem=sems.at[1],
                 device_id={"dp": r, "tensor": lane},
@@ -124,14 +125,24 @@
             return carry
 
         lax.fori_loop(1, peers, one, 0)
-        pltpu.make_async_copy(sent.at[me], rows.at[my_rows(base)], sems.at[1]).start()
-
-    deal(kv_send, kv_rows, own, kv_sems)
-    deal(q_send, q_rows, 0, q_sems)
-    deal(g_send, g_rows, 0, g_sems)
+        pltpu.make_async_copy(
+            sent.at[me, :, cols], rows.at[my_rows(base), cols], sems.at[1]
+        ).start()
+
+    def columns(group):
+        return pl.ds(group[0] * HEAD, (group[1] - group[0]) * HEAD)
 
     def arrived(rows, sems):
         pltpu.make_async_copy(rows, rows, sems.at[1]).wait()
+
+    deals = [
+        (kv_send, kv_rows, own, kv_sems, pl.ds(0, 2 * HEAD)),
+        (q_send, q_rows, 0, q_sems, pl.ds(0, width)),
+    ]
+    for n, group in enumerate(GROUPS):
+        deals.append((g_send, g_rows, 0, g_sems.at[n], columns(group)))
+    for one_deal in deals:
+        deal(*one_deal)
 
     own_kv = kv_rows.at[pl.ds(own, tok)]
     arrived(own_kv, kv_sems)
@@ -167,20 +178,16 @@
         out_buf[:, head(h)] = o.T.astype(jnp.bfloat16)
         return carry
 
+    dkv_acc[...] = jnp.zeros_like(dkv_acc)
     lax.fori_loop(0, QUERY_GROUP, forward, 0)
     out_copy = pltpu.make_async_copy(out_buf, out_hbm, out_sem.at[0])
     out_copy.start()
 
-    arrived(g_rows, g_sems)
-
-    def turn(h, carry):
+    def turn(h):
         g_f = g_rows[:, head(h)].astype(jnp.float32).T
         o_t = out_buf[:, head(h)].astype(jnp.float32).T
         gt[h] = g_f.astype(jnp.bfloat16)
         delta[h] = jnp.sum(g_f * o_t, axis=0, keepdims=True)
-        return carry
-
-    lax.fori_loop(0, QUERY_GROUP, turn, 0)
 
     def backward(n, h):
         at = pl.ds(n * tok, tok)
@@ -188,10 +195,13 @@
         dprob = dot(kv_rows[at, HEAD:], gt[h], NN)
         ds = (SCALE * pr * (dprob - delta[h])).astype(jnp.bfloat16)
         term = dot(kt[:, at], ds, NN)
-        dqt[h] = term if n == 0 else dqt[h] + term
-        dk = dot(ds, q_rows[:, head(h)], NN)
-        dv = dot(pr.astype(jnp.bfloat16), g_rows[:, head(h)], NN)
-        return dk, dv
+        total = term if n == 0 else dqt[h] + term
+        if n == NEARBY - 1:
+            dq_buf[:, head(h)] = total.T.astype(jnp.bfloat16)
+        else:
+            dqt[h] = total
+        dkv_acc[at, 0:HEAD] += dot(ds, q_rows[:, head(h)], NN)
+        dkv_acc[at, HEAD:] += dot(pr.astype(jnp.bfloat16), g_rows[:, head(h)], NN)
 
     back = []
 
@@ -207,39 +217,41 @@
         copy.start()
         back.append(copy)
 
-    for n in range(NEARBY):
-        dk, dv = backward(n, 0)
-        dkv_acc[:, 0:HEAD] = dk
-        dkv_acc[:, HEAD:] = dv
-        if n > 0:
-            send_part(n - 1)
-
-        def more(h, carry, n=n):
-            dk, dv = backward(n, h)
-            dkv_acc[:, 0:HEAD] += dk
-            dkv_acc[:, HEAD:] += dv
-            if n == NEARBY - 1:
-                dq_buf[:, head(h)] = dqt[h].T.astype(jnp.bfloat16)
+    for n, group in enumerate(GROUPS[:-1]):
+        arrived(g_rows.at[:, columns(group)], g_sems.at[n])
+
+        def whole(h, carry):
+            turn(h)
+            for m in range(NEARBY):
+                backward(m, h)
             return carry
 
-        lax.fori_loop(1, QUERY_GROUP, more, 0)
-        if n == NEARBY - 1:
-            dq_buf[:, 0:HEAD] = dqt[0].T.astype(jnp.bfloat16)
-        else:
-            part_send[n] = dkv_acc[...].astype(jnp.bfloat16)
+        lax.fori_loop(*group, whole, 0)
+
+    first, end = GROUPS[-1]
+    arrived(g_rows.at[:, columns(GROUPS[-1])], g_sems.at[len(GROUPS) - 1])
+    for h in range(first, end):
+        turn(h)
+    for m in range(NEARBY):
+        for h in range(first, end):
+            backward(m, h)
+            if h == first and m > 0:
+                send_part(m - 1)
+        if m < NEARBY - 1:
+            part_send[m] = dkv_acc[m * tok : (m + 1) * tok].astype(jnp.bfloat16)
 
     dq_copy = pltpu.make_async_copy(dq_buf, dq_hbm, out_sem.at[1])
     dq_copy.start()
     for copy in back:
         copy.wait()
-    total = dkv_acc[...]
+    total = dkv_acc[own:]
     for n in range(NEARBY - 1):
         total = total + part_recv[n].astype(jnp.float32)
     dk_ref[...] = total[:, 0:HEAD].astype(jnp.bfloat16)
     dv_ref[...] = total[:, HEAD:].astype(jnp.bfloat16)
 
-    for sent, sems in ((kv_send, kv_sems), (q_send, q_sems), (g_send, g_sems)):
-        gone = sent.at[pl.ds(0, peers - 1)]
+    for sent, _, _, sems, cols in deals:
+        gone = sent.at[pl.ds(0, peers - 1), :, cols]
         pltpu.make_async_copy(gone, gone, sems.at[0]).wait()
     out_copy.wait()
     dq_copy.wait()
@@ -305,14 +317,14 @@
                 pltpu.VMEM((QUERY_GROUP, HEAD, tok), f32),
                 pltpu.VMEM((NEARBY - 1, tok, 2 * HEAD), bf),
                 pltpu.VMEM((NEARBY - 1, tok, 2 * HEAD), bf),
-                pltpu.VMEM((tok, 2 * HEAD), f32),
+                pltpu.VMEM((NEARBY * tok, 2 * HEAD), f32),
                 pltpu.VMEM((tok, width), bf),
                 pltpu.VMEM((tok, width), bf),
                 dma((4,)),
                 dma,
                 dma((2,)),
                 dma((2,)),
-                dma((2,)),
+                dma((len(GROUPS), 2)),
                 dma((NEARBY - 1,)),
                 dma((NEARBY - 1,)),
                 dma((NEARBY - 1,)),

time: 57.7 us -> 54.1 us (0.938)
  Pallas kernels: 56.2 us -> 52.6 us
    pallas_call x1, Pallas kernels: 55.2 us -> 51.5 us  [on_device(): pl.pallas_call(functools.partial(kernel, n_dp, n_ctx, n_lane, sub), out_s...]
where the time goes in v3:
time: 54.1 us; the launch traced here: 53.9 us
  Pallas kernels  52.6 us (97%)
  local copies, waits for them, and re-layouts  0.67 us (1%)
  between operations  0.65 us (1%)
    pallas_call x1, Pallas kernels, on_device(): pl.pallas_call(functools.partial(kernel, n_dp, n_ctx, n_lane, sub), out_s...  51.5 us

profile of v3, /device:TPU:2, one launch (start us, length us, event | category | flops | bytes accessed | tf_op | source)
XLA Modules:
  0.0 53.9 jit_solution(3716940230510238757)
XLA Ops:
  0.6 0.0 copy-start
  0.6 0.7 %copy-done = s32[4,32]{1,0:T(4,128)S(1)} copy-done((s32[4,32]{1,0:T(4,128)S(1)}, s32[4,32]{1,0:T(4,128)}, u32[]{:S(2)}) %copy-start) | copy-done | bytes 536
  1.3 51.5 %shard_map.93 = (bf16[256,1024]{1,0:T(8,128)(2,1)S(1)}, bf16[256,1024]{1,0:T(8,128)(2,1)S(1)}, bf16[256,128]{1,0:T(8,128)(2,1)S(1)}, bf16[256,128]{1,0:T(8,128)(2,1)S(1)}) custom-call(bf16[4,8,8192]{2,1,0:T(8,128)(2,1)} %bitcast.5, bf16[4,8,1024]{2,1,0:T(8,128)(2,1)} %bitcast.7, bf16[4,8,1024]{2,1,0:T(8,128)(2,1)} %bitcast.8, bf16[4,8,8192]{2,1,0:T(8,128)(2,1)} %bitcast.6, ...), custom_call_target="tpu_custom_call" | custom-call | tf_op jit(solution)/shard_map/pallas_call | solution.py:289
  52.9 1.0 %shard_map.94 = (bf16[256,1024]{1,0:T(8,128)(2,1)}, bf16[256,1024]{1,0:T(8,128)(2,1)}, bf16[256,128]{1,0:T(8,128)(2,1)}, bf16[256,128]{1,0:T(8,128)(2,1)}) custom-call(bf16[256,1024]{1,0:T(8,128)(2,1)S(1)} %get-tuple-element.8.refs_0_, bf16[256,1024]{1,0:T(8,128)(2,1)S(1)} %get-tuple-element.9.refs_1_, bf16[256,128]{1,0:T(8,128)(2,1)S(1)} %get-tuple-element.10.refs_2_, ...), custom_call_target="tpu_custom_call" | custom-call | tf_op jit(solution)/shard_map/pallas_call | solution.py:338
Async XLA Ops:
  0.6 0.7 %copy-start = (s32[4,32]{1,0:T(4,128)S(1)}, s32[4,32]{1,0:T(4,128)}, u32[]{:S(2)}) copy-start(s32[4,32]{1,0:T(4,128)} %lengths.1) | copy-start | bytes 1540

commit v4 on v3

--- a/solution.py
+++ b/solution.py
@@ -11,7 +11,8 @@
 QUERY_GROUP = 8
 NEARBY = 3
 MESH = pl.DeviceIdType.MESH
-GROUPS = ((0, 4), (4, 6), (6, 8))
+Q_GROUPS = ((0, 4), (4, 8))
+G_GROUPS = ((0, 4), (4, 7), (7, 8))
 MASKED = -1e30
 SCALE = HEAD ** (-0.5)
 LOG2E = 1.4426950408889634
@@ -26,9 +27,9 @@
 
 def kernel(
     n_dp, n_ctx, n_lane, sub,
-    q_hbm, k_hbm, v_hbm, g_hbm, lengths, plan_hbm,
+    q_hbm, k_hbm, v_hbm, g_hbm, lengths_hbm, plan_hbm,
     out_hbm, dq_hbm, dk_ref, dv_ref,
-    q_in, k_in, v_in, g_in, plan,
+    q_in, k_in, v_in, g_in, lengths, plan,
     q_send, kv_send, g_send, q_rows, kv_rows, g_rows,
     bias, probs, kt, vt, gt, delta, dqt, part_send, part_recv, dkv_acc, out_buf, dq_buf,
     in_sem, plan_sem, q_sems, kv_sems, g_sems, halo_send, halo_recv, back_send, back_recv, out_sem,
@@ -62,8 +63,10 @@
     for by in (-2, -1, 1, 2):
         pl.semaphore_signal(barrier, inc=1, device_id=ctx(by), device_id_type=MESH)
 
-    plan_copy = pltpu.make_async_copy(plan_hbm.at[s], plan, plan_sem)
+    plan_copy = pltpu.make_async_copy(plan_hbm.at[s], plan, plan_sem.at[0])
     plan_copy.start()
+    lengths_copy = pltpu.make_async_copy(lengths_hbm, lengths, plan_sem.at[1])
+    lengths_copy.start()
     loads = [
         pltpu.make_async_copy(a, b, in_sem.at[n])
         for n, (a, b) in enumerate(
@@ -73,6 +76,7 @@
     for copy in loads:
         copy.start()
     plan_copy.wait()
+    lengths_copy.wait()
     for copy in loads:
         copy.wait()
 
@@ -137,9 +141,10 @@
 
     deals = [
         (kv_send, kv_rows, own, kv_sems, pl.ds(0, 2 * HEAD)),
-        (q_send, q_rows, 0, q_sems, pl.ds(0, width)),
     ]
-    for n, group in enumerate(GROUPS):
+    for n, group in enumerate(Q_GROUPS):
+        deals.append((q_send, q_rows, 0, q_sems.at[n], columns(group)))
+    for n, group in enumerate(G_GROUPS):
         deals.append((g_send, g_rows, 0, g_sems.at[n], columns(group)))
     for one_deal in deals:
         deal(*one_deal)
@@ -163,8 +168,6 @@
     kt[...] = kv_rows[:, 0:HEAD].astype(jnp.float32).T.astype(jnp.bfloat16)
     vt[...] = kv_rows[:, HEAD:].astype(jnp.float32).T.astype(jnp.bfloat16)
 
-    arrived(q_rows, q_sems)
-
     def head(h):
         return pl.ds(pl.multiple_of(h * HEAD, HEAD), HEAD)
 
@@ -179,7 +182,9 @@
         return carry
 
     dkv_acc[...] = jnp.zeros_like(dkv_acc)
-    lax.fori_loop(0, QUERY_GROUP, forward, 0)
+    for n, group in enumerate(Q_GROUPS):
+        arrived(q_rows.at[:, columns(group)], q_sems.at[n])
+        lax.fori_loop(*group, forward, 0)
     out_copy = pltpu.make_async_copy(out_buf, out_hbm, out_sem.at[0])
     out_copy.start()
 
@@ -217,7 +222,7 @@
         copy.start()
         back.append(copy)
 
-    for n, group in enumerate(GROUPS[:-1]):
+    for n, group in enumerate(G_GROUPS[:-1]):
         arrived(g_rows.at[:, columns(group)], g_sems.at[n])
 
         def whole(h, carry):
@@ -228,8 +233,8 @@
 
         lax.fori_loop(*group, whole, 0)
 
-    first, end = GROUPS[-1]
-    arrived(g_rows.at[:, columns(GROUPS[-1])], g_sems.at[len(GROUPS) - 1])
+    first, end = G_GROUPS[-1]
+    arrived(g_rows.at[:, columns(G_GROUPS[-1])], g_sems.at[len(G_GROUPS) - 1])
     for h in range(first, end):
         turn(h)
     for m in range(NEARBY):
@@ -280,11 +285,11 @@
             pltpu.with_memory_space_constraint(a.reshape(n_dp, sub, a.shape[1]), pltpu.HBM)
             for a in (queries, keys, values, grad_out)
         ]
+        lengths = pltpu.with_memory_space_constraint(doc_lengths, pltpu.HBM)
         plans = pltpu.with_memory_space_constraint(deal_plan.transpose(1, 2, 3, 0), pltpu.HBM)
         any_ = pl.BlockSpec(memory_space=pl.ANY)
         hbm = pl.BlockSpec(memory_space=pltpu.HBM)
         vmem = pl.BlockSpec(memory_space=pltpu.VMEM)
-        smem = pl.BlockSpec(memory_space=pltpu.SMEM)
         dma = pltpu.SemaphoreType.DMA
         results = pl.pallas_call(
             functools.partial(kernel, n_dp, n_ctx, n_lane, sub),
@@ -294,13 +299,14 @@
                 pltpu.VMEM((tok, HEAD), bf),
                 pltpu.VMEM((tok, HEAD), bf),
             ),
-            in_specs=[hbm, hbm, hbm, hbm, smem, hbm],
+            in_specs=[hbm] * 6,
             out_specs=(any_, any_, vmem, vmem),
             scratch_shapes=[
                 pltpu.VMEM((n_dp, sub, n_lane * width), bf),
                 pltpu.VMEM((n_dp, sub, n_lane * HEAD), bf),
                 pltpu.VMEM((n_dp, sub, n_lane * HEAD), bf),
                 pltpu.VMEM((n_dp, sub, n_lane * width), bf),
+                pltpu.SMEM(doc_lengths.shape, jnp.int32),
                 pltpu.SMEM((n_lane, n_dp, n_ctx), jnp.int32),
                 pltpu.VMEM((peers, sub, width), bf),
                 pltpu.VMEM((peers, sub, 2 * HEAD), bf),
@@ -321,10 +327,10 @@
                 pltpu.VMEM((tok, width), bf),
                 pltpu.VMEM((tok, width), bf),
                 dma((4,)),
-                dma,
                 dma((2,)),
+                dma((len(Q_GROUPS), 2)),
                 dma((2,)),
-                dma((len(GROUPS), 2)),
+                dma((len(G_GROUPS), 2)),
                 dma((NEARBY - 1,)),
                 dma((NEARBY - 1,)),
                 dma((NEARBY - 1,)),
@@ -334,7 +340,7 @@
             compiler_params=pltpu.CompilerParams(
                 collective_id=0, has_side_effects=True, vmem_limit_bytes=48 * 1024 * 1024
             ),
-        )(*split, doc_lengths, plans)
+        )(*split, lengths, plans)
         return pl.pallas_call(
             store,
             out_shape=tuple(pltpu.HBM(a.shape, a.dtype) for a in results),

time: 54.1 us -> 52.4 us (0.969)
  Pallas kernels: 52.6 us -> 51.6 us
  local copies, waits for them, and re-layouts: 0.67 us -> 0 us
    pallas_call x1, Pallas kernels: 51.5 us -> 50.6 us  [on_device(): pl.pallas_call(functools.partial(kernel, n_dp, n_ctx, n_lane, sub), out_s...]
    unnamed x2 -> x0, local copies, waits for them, and re-layouts: 0.67 us -> none
where the time goes in v4:
time: 52.4 us; the launch traced here: 52.2 us
  Pallas kernels  51.6 us (98%)
  between operations  0.64 us (1%)
    pallas_call x1, Pallas kernels, on_device(): pl.pallas_call(functools.partial(kernel, n_dp, n_ctx, n_lane, sub), out_s...  50.6 us

profile of v4, /device:TPU:2, one launch (start us, length us, event | category | flops | bytes accessed | tf_op | source)
XLA Modules:
  0.0 52.2 jit_solution(1773899355074337310)
XLA Ops:
  0.6 50.6 %shard_map.93 = (bf16[256,1024]{1,0:T(8,128)(2,1)S(1)}, bf16[256,1024]{1,0:T(8,128)(2,1)S(1)}, bf16[256,128]{1,0:T(8,128)(2,1)S(1)}, bf16[256,128]{1,0:T(8,128)(2,1)S(1)}) custom-call(bf16[4,8,8192]{2,1,0:T(8,128)(2,1)} %bitcast.5, bf16[4,8,1024]{2,1,0:T(8,128)(2,1)} %bitcast.7, bf16[4,8,1024]{2,1,0:T(8,128)(2,1)} %bitcast.8, bf16[4,8,8192]{2,1,0:T(8,128)(2,1)} %bitcast.6, ...), custom_call_target="tpu_custom_call" | custom-call | tf_op jit(solution)/shard_map/pallas_call | solution.py:294
  51.2 1.0 %shard_map.94 = (bf16[256,1024]{1,0:T(8,128)(2,1)}, bf16[256,1024]{1,0:T(8,128)(2,1)}, bf16[256,128]{1,0:T(8,128)(2,1)}, bf16[256,128]{1,0:T(8,128)(2,1)}) custom-call(bf16[256,1024]{1,0:T(8,128)(2,1)S(1)} %get-tuple-element.8.refs_0_, bf16[256,1024]{1,0:T(8,128)(2,1)S(1)} %get-tuple-element.9.refs_1_, bf16[256,128]{1,0:T(8,128)(2,1)S(1)} %get-tuple-element.10.refs_2_, ...), custom_call_target="tpu_custom_call" | custom-call | tf_op jit(solution)/shard_map/pallas_call | solution.py:344

commit v5 on v4

--- a/solution.py
+++ b/solution.py
@@ -12,7 +12,7 @@
 NEARBY = 3
 MESH = pl.DeviceIdType.MESH
 Q_GROUPS = ((0, 4), (4, 8))
-G_GROUPS = ((0, 4), (4, 7), (7, 8))
+G_GROUPS = ((0, 4), (4, 6), (6, 7), (7, 8))
 MASKED = -1e30
 SCALE = HEAD ** (-0.5)
 LOG2E = 1.4426950408889634

time: 52.4 us -> 52.4 us (level)
  no operation moved by 1% of the time
where the time goes in v5:
time: 52.4 us; the launch traced here: 52.2 us
  Pallas kernels  51.6 us (98%)
  between operations  0.64 us (1%)
    pallas_call x1, Pallas kernels, on_device(): pl.pallas_call(functools.partial(kernel, n_dp, n_ctx, n_lane, sub), out_s...  50.6 us

profile of v5, /device:TPU:2, one launch (start us, length us, event | category | flops | bytes accessed | tf_op | source)
XLA Modules:
  0.0 52.2 jit_solution(1484521977139921296)
XLA Ops:
  0.6 50.6 %shard_map.93 = (bf16[256,1024]{1,0:T(8,128)(2,1)S(1)}, bf16[256,1024]{1,0:T(8,128)(2,1)S(1)}, bf16[256,128]{1,0:T(8,128)(2,1)S(1)}, bf16[256,128]{1,0:T(8,128)(2,1)S(1)}) custom-call(bf16[4,8,8192]{2,1,0:T(8,128)(2,1)} %bitcast.5, bf16[4,8,1024]{2,1,0:T(8,128)(2,1)} %bitcast.7, bf16[4,8,1024]{2,1,0:T(8,128)(2,1)} %bitcast.8, bf16[4,8,8192]{2,1,0:T(8,128)(2,1)} %bitcast.6, ...), custom_call_target="tpu_custom_call" | custom-call | tf_op jit(solution)/shard_map/pallas_call | solution.py:294
  51.2 1.0 %shard_map.94 = (bf16[256,1024]{1,0:T(8,128)(2,1)}, bf16[256,1024]{1,0:T(8,128)(2,1)}, bf16[256,128]{1,0:T(8,128)(2,1)}, bf16[256,128]{1,0:T(8,128)(2,1)}) custom-call(bf16[256,1024]{1,0:T(8,128)(2,1)S(1)} %get-tuple-element.8.refs_0_, bf16[256,1024]{1,0:T(8,128)(2,1)S(1)} %get-tuple-element.9.refs_1_, bf16[256,128]{1,0:T(8,128)(2,1)S(1)} %get-tuple-element.10.refs_2_, ...), custom_call_target="tpu_custom_call" | custom-call | tf_op jit(solution)/shard_map/pallas_call | solution.py:344

commit v6 on v4

--- a/solution.py
+++ b/solution.py
@@ -146,7 +146,7 @@
         deals.append((q_send, q_rows, 0, q_sems.at[n], columns(group)))
     for n, group in enumerate(G_GROUPS):
         deals.append((g_send, g_rows, 0, g_sems.at[n], columns(group)))
-    for one_deal in deals:
+    for one_deal in deals[:2]:
         deal(*one_deal)
 
     own_kv = kv_rows.at[pl.ds(own, tok)]
@@ -163,6 +163,8 @@
         )
         copy.start()
         halo.append(copy)
+    for one_deal in deals[2:]:
+        deal(*one_deal)
     for copy in halo:
         copy.wait()
     kt[...] = kv_rows[:, 0:HEAD].astype(jnp.float32).T.astype(jnp.bfloat16)

time: 52.4 us -> 52.3 us (level)
  no operation moved by 1% of the time
where the time goes in v6:
time: 52.3 us; the launch traced here: 52.2 us
  Pallas kernels  51.5 us (98%)
  between operations  0.64 us (1%)
    pallas_call x1, Pallas kernels, on_device(): pl.pallas_call(functools.partial(kernel, n_dp, n_ctx, n_lane, sub), out_s...  50.5 us

profile of v6, /device:TPU:2, one launch (start us, length us, event | category | flops | bytes accessed | tf_op | source)
XLA Modules:
  0.0 52.2 jit_solution(16275692467863346778)
XLA Ops:
  0.6 50.5 %shard_map.93 = (bf16[256,1024]{1,0:T(8,128)(2,1)S(1)}, bf16[256,1024]{1,0:T(8,128)(2,1)S(1)}, bf16[256,128]{1,0:T(8,128)(2,1)S(1)}, bf16[256,128]{1,0:T(8,128)(2,1)S(1)}) custom-call(bf16[4,8,8192]{2,1,0:T(8,128)(2,1)} %bitcast.5, bf16[4,8,1024]{2,1,0:T(8,128)(2,1)} %bitcast.7, bf16[4,8,1024]{2,1,0:T(8,128)(2,1)} %bitcast.8, bf16[4,8,8192]{2,1,0:T(8,128)(2,1)} %bitcast.6, ...), custom_call_target="tpu_custom_call" | custom-call | tf_op jit(solution)/shard_map/pallas_call | solution.py:296
  51.2 1.0 %shard_map.94 = (bf16[256,1024]{1,0:T(8,128)(2,1)}, bf16[256,1024]{1,0:T(8,128)(2,1)}, bf16[256,128]{1,0:T(8,128)(2,1)}, bf16[256,128]{1,0:T(8,128)(2,1)}) custom-call(bf16[256,1024]{1,0:T(8,128)(2,1)S(1)} %get-tuple-element.8.refs_0_, bf16[256,1024]{1,0:T(8,128)(2,1)S(1)} %get-tuple-element.9.refs_1_, bf16[256,128]{1,0:T(8,128)(2,1)S(1)} %get-tuple-element.10.refs_2_, ...), custom_call_target="tpu_custom_call" | custom-call | tf_op jit(solution)/shard_map/pallas_call | solution.py:346
